TPU v7x, 256 devices: a whole 4x4x8 slice. The times are simulated.
256 devices in a mesh: blk: 8 (over y_hi, x), head: 8 (over z), bend: 4 (over y_lo, core).
Axes of the slice: x: 4, y: 4 (y_hi: 2, y_lo: 2; y = y_hi * 2 + y_lo), z: 8, core: 2. Of those that a mesh axis runs over, the one named last changes fastest.
Arguments:
- queries: bfloat16 [65536, 768], P(('bend', 'blk', 'head')), parts along dimension 0, may hold values from -9 to 9
- keys_values: bfloat16 [2, 65536, 768], P(None, ('bend', 'blk', 'head')), parts along dimension 1, may hold values from -6 to 6
- surface: bfloat16 [65536, 768], P(('bend', 'blk', 'head')), parts along dimension 0, may hold values from -6 to 6
- out_weight: bfloat16 [768, 768], P('head'), may hold values from -0.21875 to 0.21875
- up_weight: bfloat16 [768, 3072], P('head'), may hold values from -0.21875 to 0.21875
- down_weight: bfloat16 [3072, 768], P('head'), may hold values from -0.109375 to 0.109375
- norm_gain: float32 [768], replicated, may hold values from 0.25 to 1.75
- block_lists: int32 [256, 4], P(('bend', 'blk', 'head')), parts along dimension 0, may hold values from 0 to 63, as said below
- list_lengths: int32 [256], P(('bend', 'blk', 'head')), parts along dimension 0, may hold values from 1 to 4
Outputs:
- mixed_out: bfloat16 [65536, 768], P(('bend', 'blk', 'head')), parts along dimension 0
There are 4 independent parts, one for each index of `bend`. A program takes and returns all parts, laid end to end along the dimension named above; an argument that names none is the same for every part. Nothing has to cross between parts.
Inputs may be any that keep to these rules, and one draw needn't show every extreme that they name: `block_lists`: the list of query block b holds distinct anchor blocks, all within cycle distance 3 (modulo 64) of anchor block b, and its first entry is that block itself.
All inputs are finite; a program needn't handle non-finite values.
Results may differ from a plain program's by a relative error of at most 0.0065.
Values may be sent and summed in bfloat16 or wider, within the bound.
A program may use at most 128 MiB of HBM per device.

v0:
```python
import jax
import jax.numpy as jnp
from jax import lax
from jax.sharding import PartitionSpec as P

HEADS = 12
HD = 64
LIST = 4


def passed_along(block, axis, distance):
    devices = range(lax.axis_size(axis))
    route = [((i - distance) % len(devices), i) for i in devices]
    return lax.ppermute(block, axis, route)


def fold_rows(running, left_side, portion):
    return running + jnp.dot(left_side, portion, preferred_element_type=jnp.float32)


def shards(
    queries,
    keys_values,
    surface,
    out_weight,
    up_weight,
    down_weight,
    norm_gain,
    block_lists,
    list_lengths,
):
    row_count, feature_width = queries.shape
    query_blocks = block_lists.shape[0]
    block_rows = row_count // query_blocks
    loop_size = lax.axis_size(("blk", "head"))
    cycle_reach = min(3, (loop_size - 1) // 2)
    own_index = lax.axis_index(("blk", "head"))
    query_heads = queries.reshape(query_blocks, block_rows, HEADS, HD)
    score_scale = 1.0 / HD**0.5
    entry_live = jnp.arange(LIST, dtype=jnp.int32)[None, :] < list_lengths[:, None]
    start_state = (
        jnp.full((query_blocks, HEADS, block_rows), -1e30, jnp.float32),
        jnp.zeros((query_blocks, HEADS, block_rows), jnp.float32),
        jnp.zeros((query_blocks, HEADS, block_rows, HD), jnp.float32),
    )

    def absorb(softmax_state, anchor_pair, source):
        listed = jnp.any((block_lists == source) & entry_live, axis=1)
        running_max, running_sum, running_acc = softmax_state
        block_keys = anchor_pair[0].reshape(block_rows, HEADS, HD)
        block_values = anchor_pair[1].reshape(block_rows, HEADS, HD)
        scores = (
            jnp.einsum(
                "bqhd,khd->bhqk", query_heads, block_keys, preferred_element_type=jnp.float32
            )
            * score_scale
        )
        block_max = jnp.max(scores, axis=3)
        new_max = jnp.where(listed[:, None, None], jnp.maximum(running_max, block_max), running_max)
        ratio = jnp.exp(running_max - new_max)
        weights_exp = jnp.where(
            listed[:, None, None, None], jnp.exp(scores - new_max[..., None]), 0.0
        )
        new_sum = running_sum * ratio + jnp.sum(weights_exp, axis=3)
        probs = weights_exp.astype(jnp.bfloat16)
        new_acc = running_acc * ratio[..., None] + jnp.einsum(
            "bhqk,khd->bhqd", probs, block_values, preferred_element_type=jnp.float32
        )
        return (new_max, new_sum, new_acc)

    moving = passed_along(keys_values, ("blk", "head"), -cycle_reach)
    source = (own_index + cycle_reach) % loop_size
    softmax_state = absorb(start_state, moving, source)
    for cycle_turn in range(2 * cycle_reach):
        moving = passed_along(moving, ("blk", "head"), 1)
        source = (source - 1) % loop_size
        softmax_state = absorb(softmax_state, moving, source)
    final_max, final_sum, final_acc = softmax_state
    context = final_acc / final_sum[..., None]
    context = (
        jnp.transpose(context, (0, 2, 1, 3)).reshape(row_count, feature_width).astype(jnp.bfloat16)
    )
    residual = surface.astype(jnp.float32)
    hidden = fold_rows(residual, context, lax.all_gather(out_weight, "head", axis=0, tiled=True))
    mean_square = jnp.mean(hidden * hidden, axis=1, keepdims=True)
    normed = (hidden * lax.rsqrt(mean_square + 1e-05) * norm_gain[None, :]).astype(jnp.bfloat16)
    up_start = jnp.zeros((row_count, up_weight.shape[1]), jnp.float32)
    pre_gelu = fold_rows(up_start, normed, lax.all_gather(up_weight, "head", axis=0, tiled=True))
    activated = jax.nn.gelu(pre_gelu, approximate=True).astype(jnp.bfloat16)
    mixed_out = fold_rows(
        hidden, activated, lax.all_gather(down_weight, "head", axis=0, tiled=True)
    )
    return mixed_out.astype(jnp.bfloat16)


def solution(mesh):
    return jax.shard_map(
        shards,
        mesh=mesh,
        in_specs=(
            P(("bend", "blk", "head"), None),
            P(None, ("bend", "blk", "head"), None),
            P(("bend", "blk", "head"), None),
            P("head", None),
            P("head", None),
            P("head", None),
            P(),
            P(("bend", "blk", "head"), None),
            P(("bend", "blk", "head")),
        ),
        out_specs=P(("bend", "blk", "head"), None),
        check_vma=False,
    )
```

profile of v0, /device:TPU:8, one launch (start us, length us, event | category | flops | bytes accessed | tf_op | source)
XLA Modules:
  0.0 336.4 jit_solution(10277516202855347654)
XLA Ops:
  8.1 10.7 %collective-permute-start = (bf16[2,256,768]{2,1,0:T(8,128)(2,1)}, bf16[2,256,768]{2,1,0:T(8,128)(2,1)S(1)}, u32[]{:S(2)}, u32[]{:S(2)}) collective-permute-start(bf16[2,256,768]{2,1,0:T(8,128)(2,1)} %param.10), channel_id=1, source_target_pairs={{12,0},{16,4},{20,8},{24,12},{28,16},{32,20},{36,24},{40,28},{44,3... | collective-permute-start | bytes 2359304 | tf_op jit(solution)/shard_map/ppermute | solution.py:14
  18.8 61.9 %collective-permute-done = bf16[2,256,768]{2,1,0:T(8,128)(2,1)S(1)} collective-permute-done((bf16[2,256,768]{2,1,0:T(8,128)(2,1)}, bf16[2,256,768]{2,1,0:T(8,128)(2,1)S(1)}, u32[]{:S(2)}, u32[]{:S(2)}) %collective-permute-start) | collective-permute-done | bytes 786464 | tf_op jit(solution)/shard_map/ppermute | solution.py:14
  80.7 37.6 %collective-permute-done.1 = bf16[2,256,768]{2,1,0:T(8,128)(2,1)S(1)} collective-permute-done((bf16[2,256,768]{2,1,0:T(8,128)(2,1)S(1)}, bf16[2,256,768]{2,1,0:T(8,128)(2,1)S(1)}, u32[]{:S(2)}, u32[]{:S(2)}) %collective-permute-start.1) | collective-permute-done | bytes 786464 | tf_op jit(solution)/shard_map/ppermute | solution.py:14
  119.1 1.2 copy.39
  120.3 1.4 and_reduce_fusion
  121.7 37.8 %collective-permute-done.2 = bf16[2,256,768]{2,1,0:T(8,128)(2,1)S(1)} collective-permute-done((bf16[2,256,768]{2,1,0:T(8,128)(2,1)S(1)}, bf16[2,256,768]{2,1,0:T(8,128)(2,1)S(1)}, u32[]{:S(2)}, u32[]{:S(2)}) %collective-permute-start.2) | collective-permute-done | bytes 786464 | tf_op jit(solution)/shard_map/ppermute | solution.py:14
  159.5 1.5 fusion.203
  162.1 2.8 bitcast_reduce_fusion.6
  166.8 16.6 %collective-permute-done.3 = bf16[2,256,768]{2,1,0:T(8,128)(2,1)} collective-permute-done((bf16[2,256,768]{2,1,0:T(8,128)(2,1)S(1)}, bf16[2,256,768]{2,1,0:T(8,128)(2,1)}, u32[]{:S(2)}, u32[]{:S(2)}) %collective-permute-start.3) | collective-permute-done | bytes 786464 | tf_op jit(solution)/shard_map/ppermute | solution.py:14
  183.5 2.2 bitcast_reduce_fusion.5
  186.6 2.0 copy.45
  188.6 1.9 copy.46
  190.5 3.3 bitcast_reduce_fusion.4
  193.8 28.9 %collective-permute-done.4 = bf16[2,256,768]{2,1,0:T(8,128)(2,1)} collective-permute-done((bf16[2,256,768]{2,1,0:T(8,128)(2,1)}, bf16[2,256,768]{2,1,0:T(8,128)(2,1)}, u32[]{:S(2)}, u32[]{:S(2)}) %collective-permute-start.4) | collective-permute-done | bytes 786464 | tf_op jit(solution)/shard_map/ppermute | solution.py:14
  222.7 2.1 fusion.200
  224.8 1.9 copy.48
  226.7 1.9 copy.49
  228.7 3.9 %bitcast_reduce_fusion.3 = (f32[12,256]{1,0:T(8,128)}, f32[12,256,256]{2,1,0:T(8,128)}) fusion(bf16[256,12,64]{0,2,1:T(8,128)(2,1)} %bitcast.450, bf16[256,12,64]{0,2,1:T(8,128)(2,1)S(1)} %bitcast.436), kind=kOutput, calls=%fused_computation.22 | convolution fusion | flops 102233088 | bytes 3944448 | tf_op jit(solution)/shard_map/bqhd,khd->bhqk/dot_general | solution.py:53
  232.5 2.1 fusion.199
  234.6 1.9 copy.51
  236.5 1.9 copy.52
  238.5 24.6 %collective-permute-done.5 = bf16[2,256,768]{2,1,0:T(8,128)(2,1)} collective-permute-done((bf16[2,256,768]{2,1,0:T(8,128)(2,1)}, bf16[2,256,768]{2,1,0:T(8,128)(2,1)}, u32[]{:S(2)}, u32[]{:S(2)}) %collective-permute-start.5) | collective-permute-done | bytes 786464 | tf_op jit(solution)/shard_map/ppermute | solution.py:14
  263.1 3.9 %bitcast_reduce_fusion.2 = (f32[12,256]{1,0:T(8,128)}, f32[12,256,256]{2,1,0:T(8,128)}) fusion(bf16[256,12,64]{0,2,1:T(8,128)(2,1)} %bitcast.445, bf16[256,12,64]{0,2,1:T(8,128)(2,1)S(1)} %bitcast.437), kind=kOutput, calls=%fused_computation.18 | convolution fusion | flops 102233088 | bytes 3944448 | tf_op jit(solution)/shard_map/bqhd,khd->bhqk/dot_general | solution.py:53
  267.0 2.1 fusion.198
  269.1 2.0 copy.54
  271.0 1.9 copy.55
  273.0 3.9 %bitcast_reduce_fusion.1 = (f32[12,256]{1,0:T(8,128)}, f32[12,256,256]{2,1,0:T(8,128)}) fusion(bf16[256,12,64]{0,2,1:T(8,128)(2,1)} %bitcast.451, bf16[256,12,64]{0,2,1:T(8,128)(2,1)S(1)} %bitcast.438), kind=kOutput, calls=%fused_computation.14 | convolution fusion | flops 102233088 | bytes 3944448 | tf_op jit(solution)/shard_map/bqhd,khd->bhqk/dot_general | solution.py:53
  276.8 7.8 %collective-permute-done.6 = bf16[2,256,768]{2,1,0:T(8,128)(2,1)} collective-permute-done((bf16[2,256,768]{2,1,0:T(8,128)(2,1)}, bf16[2,256,768]{2,1,0:T(8,128)(2,1)}, u32[]{:S(2)}, u32[]{:S(2)}) %collective-permute-start.6) | collective-permute-done | bytes 786464 | tf_op jit(solution)/shard_map/ppermute | solution.py:14
  284.6 2.0 fusion.197
  286.7 1.9 copy.57
  288.6 1.9 copy.58
  290.6 1.8 bitcast_reduce_fusion
  292.4 4.2 %maximum_select_fusion = (f32[12,256]{1,0:T(8,128)S(1)}, f32[12,256]{1,0:T(8,128)S(1)}, f32[12,256]{1,0:T(8,128)S(1)}, f32[12,256]{1,0:T(8,128)S(1)}, f32[12,256...) fusion(f32[12,256]{1,0:T(8,128)S(1)} %get-tuple-element.42, pred[]{:T(512)} %get-tuple-element.5, ...), kind=kLoop, calls=%fused_computation.128 | loop fusion | flops 43008 | bytes 172039 | tf_op jit(solution)/shard_map/jit(_where)/select_n | solution.py:59
  296.6 1.8 maximum_select_fusion.6
  298.5 1.2 fusion.34
  299.7 3.0 fusion.22
  302.7 3.0 fusion.26
  305.7 2.5 fusion.30
  308.3 2.4 bitcast_add_fusion
  310.7 1.2 fusion.148
  312.0 1.4 fusion.142
  313.4 1.3 fusion.136
  314.7 1.4 fusion.130
  316.1 1.4 fusion.124
  317.5 1.3 fusion.118
  318.8 1.3 fusion.160
  320.2 2.1 multiply_reduce_fusion
  322.3 7.5 %fusion.154 = bf16[256,768]{1,0:T(8,128)(2,1)} fusion(f32[256,768]{1,0:T(8,128)S(1)} %get-tuple-element.57, bf16[3072,768]{1,0:T(8,128)(2,1)} %all-gather.8.cloned.1.call-done, bf16[768,3072]{1,0:T(8,128)(2,1)} %all-gather.6.cloned.1.call-done, f32[768]{0:T(1024)S(1)} %copy-done.21, f32[256]{0:T(256)S(1)} %add_rsqrt_fusion), kind=kOutput, calls=%fused_computation.120 | convolution fusion | flops 2423980032 | bytes 10620928 | tf_op jit(solution)/shard_map/dot_general | solution.py:18
  (67 shorter events, 5.6 us)
Async XLA Ops:
  6.5 313.6 %all-gather.4.cloned.1.call-start = ((), (), s32[]{:S(2)}) async-start(), calls=%async_computation | async-start | bytes 1327104 | tf_op jit(solution)/shard_map/all_gather | solution.py:84
  7.3 315.0 %all-gather.6.cloned.1.call-start = ((), (), s32[]{:S(2)}) async-start(), calls=%async_computation.1 | async-start | bytes 5308416 | tf_op jit(solution)/shard_map/all_gather | solution.py:88
  8.0 314.3 %all-gather.8.cloned.1.call-start = ((), (), s32[]{:S(2)}) async-start(), calls=%async_computation.2 | async-start | bytes 5308416 | tf_op jit(solution)/shard_map/all_gather | solution.py:91
  8.1 72.6 %collective-permute-start = (bf16[2,256,768]{2,1,0:T(8,128)(2,1)}, bf16[2,256,768]{2,1,0:T(8,128)(2,1)S(1)}, u32[]{:S(2)}, u32[]{:S(2)}) collective-permute-start(bf16[2,256,768]{2,1,0:T(8,128)(2,1)} %param.10), channel_id=1, source_target_pairs={{12,0},{16,4},{20,8},{24,12},{28,16},{32,20},{36,24},{40,28},{44,3... | collective-permute-start | bytes 2359304 | tf_op jit(solution)/shard_map/ppermute | solution.py:14
  80.7 37.6 %copy-start.12 = (bf16[2,256,768]{2,1,0:T(8,128)(2,1)}, bf16[2,256,768]{2,1,0:T(8,128)(2,1)S(1)}, u32[]{:S(2)}) copy-start(bf16[2,256,768]{2,1,0:T(8,128)(2,1)S(1)} %collective-permute-done) | copy-start | bytes 2359300
  80.7 37.6 %collective-permute-start.1 = (bf16[2,256,768]{2,1,0:T(8,128)(2,1)S(1)}, bf16[2,256,768]{2,1,0:T(8,128)(2,1)S(1)}, u32[]{:S(2)}, u32[]{:S(2)}) collective-permute-start(bf16[2,256,768]{2,1,0:T(8,128)(2,1)S(1)} %collective-permute-done), channel_id=1, source_target_pairs={{252,0},{0,4},{4,8},{8,12},{12,16},{16,20},{20,24},{24,28},{28,32}... | collective-permute-start | bytes 2359304 | tf_op jit(solution)/shard_map/ppermute | solution.py:14
  118.3 41.2 %collective-permute-start.2 = (bf16[2,256,768]{2,1,0:T(8,128)(2,1)S(1)}, bf16[2,256,768]{2,1,0:T(8,128)(2,1)S(1)}, u32[]{:S(2)}, u32[]{:S(2)}) collective-permute-start(bf16[2,256,768]{2,1,0:T(8,128)(2,1)S(1)} %collective-permute-done.1), channel_id=1, source_target_pairs={{252,0},{0,4},{4,8},{8,12},{12,16},{16,20},{20,24},{24,28},{28,32}... | collective-permute-start | bytes 2359304 | tf_op jit(solution)/shard_map/ppermute | solution.py:14
  159.5 5.4 %copy-start.10 = (bf16[2,256,768]{2,1,0:T(8,128)(2,1)}, bf16[2,256,768]{2,1,0:T(8,128)(2,1)S(1)}, u32[]{:S(2)}) copy-start(bf16[2,256,768]{2,1,0:T(8,128)(2,1)S(1)} %collective-permute-done.2) | copy-start | bytes 2359300
  159.5 24.0 %collective-permute-start.3 = (bf16[2,256,768]{2,1,0:T(8,128)(2,1)S(1)}, bf16[2,256,768]{2,1,0:T(8,128)(2,1)}, u32[]{:S(2)}, u32[]{:S(2)}) collective-permute-start(bf16[2,256,768]{2,1,0:T(8,128)(2,1)S(1)} %collective-permute-done.2), channel_id=1, source_target_pairs={{252,0},{0,4},{4,8},{8,12},{12,16},{16,20},{20,24},{24,28},{28,32}... | collective-permute-start | bytes 2359304 | tf_op jit(solution)/shard_map/ppermute | solution.py:14
  166.8 18.9 %copy-start.11 = (bf16[2,256,768]{2,1,0:T(8,128)(2,1)S(1)}, bf16[2,256,768]{2,1,0:T(8,128)(2,1)}, u32[]{:S(2)}) copy-start(bf16[2,256,768]{2,1,0:T(8,128)(2,1)} %copy-done.10) | copy-start | bytes 2359300
  183.5 39.3 %collective-permute-start.4 = (bf16[2,256,768]{2,1,0:T(8,128)(2,1)}, bf16[2,256,768]{2,1,0:T(8,128)(2,1)}, u32[]{:S(2)}, u32[]{:S(2)}) collective-permute-start(bf16[2,256,768]{2,1,0:T(8,128)(2,1)} %collective-permute-done.3), channel_id=1, source_target_pairs={{252,0},{0,4},{4,8},{8,12},{12,16},{16,20},{20,24},{24,28},{28,32}... | collective-permute-start | bytes 2359304 | tf_op jit(solution)/shard_map/ppermute | solution.py:14
  222.7 40.4 %collective-permute-start.5 = (bf16[2,256,768]{2,1,0:T(8,128)(2,1)}, bf16[2,256,768]{2,1,0:T(8,128)(2,1)}, u32[]{:S(2)}, u32[]{:S(2)}) collective-permute-start(bf16[2,256,768]{2,1,0:T(8,128)(2,1)} %collective-permute-done.4), channel_id=1, source_target_pairs={{252,0},{0,4},{4,8},{8,12},{12,16},{16,20},{20,24},{24,28},{28,32}... | collective-permute-start | bytes 2359304 | tf_op jit(solution)/shard_map/ppermute | solution.py:14
  263.1 21.6 %collective-permute-start.6 = (bf16[2,256,768]{2,1,0:T(8,128)(2,1)}, bf16[2,256,768]{2,1,0:T(8,128)(2,1)}, u32[]{:S(2)}, u32[]{:S(2)}) collective-permute-start(bf16[2,256,768]{2,1,0:T(8,128)(2,1)} %collective-permute-done.5), channel_id=1, source_target_pairs={{252,0},{0,4},{4,8},{8,12},{12,16},{16,20},{20,24},{24,28},{28,32}... | collective-permute-start | bytes 2359304 | tf_op jit(solution)/shard_map/ppermute | solution.py:14
  290.5 1.8 copy-start.16
  290.5 1.8 copy-start.17
  290.5 1.8 copy-start.18
  290.5 1.8 copy-start.19
  290.5 1.8 copy-start.20
  290.6 9.1 %copy-start.4 = (f32[12,256,256]{2,1,0:T(8,128)S(1)}, f32[12,256,256]{2,1,0:T(8,128)}, u32[]{:S(2)}) copy-start(f32[12,256,256]{2,1,0:T(8,128)} %get-tuple-element.55) | copy-start | bytes 9437188
  299.7 3.0 copy-start
  299.7 3.0 copy-start.1
  302.7 3.0 copy-start.2
  302.7 3.0 copy-start.3
  305.7 5.0 %copy-start.14 = (bf16[1,256,768]{1,2,0:T(8,128)(2,1)S(1)}, bf16[1,256,768]{1,2,0:T(8,128)(2,1)}, u32[]{:S(2)}) copy-start(bf16[1,256,768]{1,2,0:T(8,128)(2,1)} %copy.40) | copy-start | bytes 1179652
  308.3 3.7 %copy-start.5 = (bf16[1,256,768]{1,2,0:T(8,128)(2,1)S(1)}, bf16[1,256,768]{1,2,0:T(8,128)(2,1)}, u32[]{:S(2)}) copy-start(bf16[1,256,768]{1,2,0:T(8,128)(2,1)} %copy.43) | copy-start | bytes 1179652
  312.0 1.4 copy-start.6
  313.4 1.3 copy-start.7
  314.7 1.4 copy-start.8
  316.1 1.4 copy-start.9
  317.5 1.3 copy-start.15
  318.8 1.4 copy-start.13
  318.8 3.5 %copy-start.21 = (f32[768]{0:T(1024)S(1)}, f32[768]{0:T(1024)}, u32[]{:S(2)}) copy-start(f32[768]{0:T(1024)} %param.15) | copy-start | bytes 9220
Sparse Core Ops, SparseCore 0:
  9.1 68.3 all-gather.3
  79.3 92.9 all-gather.5
  174.1 97.4 all-gather.7
where the time goes:
time: 338 us; the launch traced here: 336 us
  waiting for transfers between devices  217 us (64%)
  matrix products  40.7 us (12%)
  local copies, waits for them, and re-layouts  34.3 us (10%)
  other arithmetic  19.6 us (6%)
  between operations  14.3 us (4%)
  starting transfers between devices  10.8 us (3%)
    ppermute x7, waiting for transfers between devices, passed_along(): return lax.ppermute(block, axis, route)  215 us
    dot_general x7, matrix products, absorb(): jnp.einsum('bqhd,khd->bhqk', query_heads, block_keys, preferred_element_t...  21.8 us
    slice x13, local copies, waits for them, and re-layouts, absorb(): block_values = anchor_pair[1].reshape(block_rows, HEADS, HD)  20.7 us
    slice x8, local copies, waits for them, and re-layouts, absorb(): block_keys = anchor_pair[0].reshape(block_rows, HEADS, HD)  12.3 us
    ppermute x7, starting transfers between devices, passed_along(): return lax.ppermute(block, axis, route)  10.8 us
    reduce_sum x4, other arithmetic, absorb(): new_sum = running_sum * ratio + jnp.sum(weights_exp, axis=3)  9.68 us
    dot_general x2, matrix products, fold_rows(): jnp.dot(left_side, portion, preferred_element_type=jnp.float32)  9.6 us
    dot_general x7, matrix products, absorb(): jnp.einsum('bhqk,khd->bhqd', probs, block_values, preferred_element_type=...  9.27 us
  transfers between devices with their start and end apart: 10, of which 7 were waited for; matrix products, arithmetic and copies ran while one was open for 26% of the time, Pallas kernels for 0%

commit v1 on v0

v1 whole, which is shorter than its diff:
```python
import functools

import jax
import jax.numpy as jnp
from jax import lax
from jax.experimental import pallas as pl
from jax.experimental.pallas import tpu as pltpu
from jax.sharding import PartitionSpec as P

HEADS = 12
HD = 64
LIST = 4
REACH = 3


def ring_shift(block, axis, size, distance):
    route = [(i, (i + distance) % size) for i in range(size)]
    return lax.ppermute(block, axis, route)


def x_shift(block, blk_size, x_size, distance):
    route = []
    for i in range(blk_size):
        hi, x = divmod(i, x_size)
        route.append((i, hi * x_size + (x + distance) % x_size))
    return lax.ppermute(block, "blk", route)


def core_swap(block, bend_size):
    route = [(i, i ^ 1) for i in range(bend_size)]
    return lax.ppermute(block, "bend", route)


def attention_kernel(n_blocks, mask_ref, q_ref, *refs):
    kv_refs = refs[:n_blocks]
    o_ref = refs[n_blocks]
    s_scr, m_scr, l_scr, acc_scr = refs[n_blocks + 1:]
    rows = q_ref.shape[0]
    for hh in range(2):
        cols = slice(hh * HD, (hh + 1) * HD)
        qh = q_ref[:, cols]
        m_scr[...] = jnp.full(m_scr.shape, -jnp.inf, jnp.float32)
        l_scr[...] = jnp.zeros(l_scr.shape, jnp.float32)
        acc_scr[...] = jnp.zeros(acc_scr.shape, jnp.float32)
        for j in range(n_blocks):
            @pl.when(mask_ref[j] > 0)
            def _():
                kh = kv_refs[j][0, :, cols]
                s = lax.dot_general(qh, kh, (((1,), (1,)), ((), ())),
                                    preferred_element_type=jnp.float32) * (1.0 / HD**0.5)
                s_scr[j] = s
                m_scr[...] = jnp.maximum(m_scr[...], jnp.max(s, axis=1, keepdims=True))
        for j in range(n_blocks):
            @pl.when(mask_ref[j] > 0)
            def _():
                w = jnp.exp(s_scr[j] - m_scr[...])
                l_scr[...] += jnp.sum(w, axis=1, keepdims=True)
                vh = kv_refs[j][1, :, cols]
                acc_scr[...] += jnp.dot(w.astype(jnp.bfloat16), vh,
                                        preferred_element_type=jnp.float32)
        o_ref[:, cols] = (acc_scr[...] / l_scr[...]).astype(o_ref.dtype)
    del rows


def attend(mask, q, blocks):
    rows, width = q.shape
    n_blocks = len(blocks)
    pair = 2 * HD
    grid_spec = pltpu.PrefetchScalarGridSpec(
        num_scalar_prefetch=1,
        grid=(width // pair,),
        in_specs=[pl.BlockSpec((rows, pair), lambda p, m: (0, p))]
        + [pl.BlockSpec((2, rows, pair), lambda p, m: (0, 0, p))] * n_blocks,
        out_specs=pl.BlockSpec((rows, pair), lambda p, m: (0, p)),
        scratch_shapes=[
            pltpu.VMEM((n_blocks, rows, rows), jnp.float32),
            pltpu.VMEM((rows, 1), jnp.float32),
            pltpu.VMEM((rows, 1), jnp.float32),
            pltpu.VMEM((rows, HD), jnp.float32),
        ],
    )
    return pl.pallas_call(
        functools.partial(attention_kernel, n_blocks),
        grid_spec=grid_spec,
        out_shape=jax.ShapeDtypeStruct((rows, width), jnp.bfloat16),
        cost_estimate=pl.CostEstimate(
            flops=4 * rows * rows * width * n_blocks,
            transcendentals=rows * rows * HEADS * n_blocks,
            bytes_accessed=2 * rows * width * (2 * n_blocks + 2),
        ),
    )(mask, q, *blocks)


def gather_weight_pieces(pieces, blk_size, x_size, bend_size, x, core):
    gathered = tuple(lax.all_gather(w, "head", axis=0, tiled=True) for w in pieces)
    from_left = x_shift(gathered, blk_size, x_size, 1)
    from_right = x_shift(gathered, blk_size, x_size, -1)
    tops = tuple(w[: w.shape[0] // 2] for w in from_left)
    bottoms = tuple(w[w.shape[0] // 2:] for w in from_right)
    far_top = x_shift(tops, blk_size, x_size, 1)
    far_bottom = x_shift(bottoms, blk_size, x_size, -1)
    far = tuple(jnp.concatenate([a, b], axis=0) for a, b in zip(far_top, far_bottom))
    mine = (gathered, from_left, from_right, far)
    partner = core_swap(mine, bend_size)
    absolute = jnp.arange(2 * x_size, dtype=jnp.int32)
    abs_x, abs_c = absolute // 2, absolute % 2
    dx = (abs_x - x) % x_size
    dxi = jnp.array([0, 2, 3, 1], jnp.int32)[dx]
    order = (abs_c ^ core) * 4 + dxi
    full = []
    for k in range(len(pieces)):
        stack = jnp.stack([mine[i][k] for i in range(4)] + [partner[i][k] for i in range(4)])
        stack = jnp.take(stack, order, axis=0)
        n, r, c = stack.shape
        full.append(jnp.transpose(stack, (1, 0, 2)).reshape(r, n * c))
    return full


def shards(
    queries,
    keys_values,
    surface,
    out_weight,
    up_weight,
    down_weight,
    norm_gain,
    block_lists,
    list_lengths,
):
    row_count, feature_width = queries.shape
    loop_size = lax.axis_size(("blk", "head"))
    blk_size = lax.axis_size("blk")
    bend_size = lax.axis_size("bend")
    x_size = 4
    own_index = lax.axis_index(("blk", "head"))
    x = lax.axis_index("blk") % x_size
    core = lax.axis_index("bend") % 2
    piece = x * 2 + core
    n_pieces = 2 * x_size

    def cols(w):
        width = w.shape[1] // n_pieces
        return lax.dynamic_slice_in_dim(w, piece * width, width, axis=1)

    out_full, up_full, down_full = gather_weight_pieces(
        (cols(out_weight), cols(up_weight), cols(down_weight)),
        blk_size, x_size, bend_size, x, core)

    blocks = [keys_values]
    ids = [own_index]
    left = right = keys_values
    for d in range(1, REACH + 1):
        left = ring_shift(left, ("blk", "head"), loop_size, 1)
        right = ring_shift(right, ("blk", "head"), loop_size, -1)
        blocks += [left, right]
        ids += [(own_index - d) % loop_size, (own_index + d) % loop_size]
    entry_live = jnp.arange(LIST, dtype=jnp.int32) < list_lengths[0]
    mask = jnp.stack(
        [jnp.any((block_lists[0] == b) & entry_live) for b in ids]).astype(jnp.int32)
    context = attend(mask, queries, blocks)

    hidden = surface.astype(jnp.float32) + jnp.dot(
        context, out_full, preferred_element_type=jnp.float32)
    mean_square = jnp.mean(hidden * hidden, axis=1, keepdims=True)
    normed = (hidden * lax.rsqrt(mean_square + 1e-05) * norm_gain[None, :]).astype(jnp.bfloat16)
    pre_gelu = jnp.dot(normed, up_full, preferred_element_type=jnp.float32)
    activated = jax.nn.gelu(pre_gelu, approximate=True).astype(jnp.bfloat16)
    mixed_out = hidden + jnp.dot(activated, down_full, preferred_element_type=jnp.float32)
    return mixed_out.astype(jnp.bfloat16)


def solution(mesh):
    return jax.shard_map(
        shards,
        mesh=mesh,
        in_specs=(
            P(("bend", "blk", "head"), None),
            P(None, ("bend", "blk", "head"), None),
            P(("bend", "blk", "head"), None),
            P("head", None),
            P("head", None),
            P("head", None),
            P(),
            P(("bend", "blk", "head"), None),
            P(("bend", "blk", "head")),
        ),
        out_specs=P(("bend", "blk", "head"), None),
        check_vma=False,
    )
```

time: 338 us -> 292 us (0.86)
  waiting for transfers between devices: 217 us -> 64.2 us
  blocking collectives: 0 us -> 81.7 us
  Pallas kernels: 0 us -> 31.9 us
  matrix products: 40.7 us -> 8.94 us
  starting transfers between devices: 10.8 us -> 38.5 us
  local copies, waits for them, and re-layouts: 34.3 us -> 53 us
  between operations: 14.3 us -> 1 us
  other arithmetic: 19.6 us -> 11.8 us
    ppermute x7 -> x30, waiting for transfers between devices: 215 us -> 64.2 us  [the longest x12 41.4 us: x_shift(): return lax.ppermute(block, 'blk', route)]
    all_gather x0 -> x3, blocking collectives: none -> 81.7 us  [gather_weight_pieces(): lax.all_gather(w, 'head', axis=0, tiled=True)]
    pallas_call x0 -> x1, Pallas kernels: none -> 31.9 us  [attend(): pl.pallas_call(functools.partial(attention_kernel, n_blocks), grid_spec=g...]
    dot_general x16 -> x2, matrix products: 40.7 us -> 8.94 us  [the longest x1 7.35 us: shards(): jnp.dot(activated, down_full, preferred_element_type=jnp.float32)]
    slice x21 -> x6, local copies, waits for them, and re-layouts: 33 us -> 3.96 us  [the longest x3 1.98 us: gather_weight_pieces(): bottoms = tuple((w[w.shape[0] // 2:] for w in from_right))]
    ppermute x7 -> x30, starting transfers between devices: 10.8 us -> 38.5 us  [the longest x12 20 us: x_shift(): return lax.ppermute(block, 'blk', route)]
    unnamed x45 -> x37, local copies, waits for them, and re-layouts: 1.27 us -> 20.9 us
    gather x0 -> x4, local copies, waits for them, and re-layouts: none -> 13.1 us  [the longest x3 11.8 us: gather_weight_pieces(): stack = jnp.take(stack, order, axis=0)]
  transfers between devices with their start and end apart: 10 -> 30, of which waited for: 7 -> 13; matrix products, arithmetic and copies ran while one was open for 26% -> 22% of each run, Pallas kernels for 0% -> 0%
where the time goes in v1:
time: 292 us; the launch traced here: 291 us
  blocking collectives  81.7 us (28%)
  waiting for transfers between devices  64.2 us (22%)
  local copies, waits for them, and re-layouts  53 us (18%)
  starting transfers between devices  38.5 us (13%)
  Pallas kernels  31.9 us (11%)
  other arithmetic  11.8 us (4%)
  matrix products  8.94 us (3%)
    all_gather x3, blocking collectives, gather_weight_pieces(): lax.all_gather(w, 'head', axis=0, tiled=True)  81.7 us
    ppermute x12, waiting for transfers between devices, x_shift(): return lax.ppermute(block, 'blk', route)  41.4 us
    pallas_call x1, Pallas kernels, attend(): pl.pallas_call(functools.partial(attention_kernel, n_blocks), grid_spec=g...  31.9 us
    unnamed x37, local copies, waits for them, and re-layouts  20.9 us
    ppermute x12, starting transfers between devices, x_shift(): return lax.ppermute(block, 'blk', route)  20 us
    ppermute x6, waiting for transfers between devices, ring_shift(): return lax.ppermute(block, axis, route)  17.9 us
    ppermute x6, starting transfers between devices, ring_shift(): return lax.ppermute(block, axis, route)  16.4 us
    gather x3, local copies, waits for them, and re-layouts, gather_weight_pieces(): stack = jnp.take(stack, order, axis=0)  11.8 us
  transfers between devices with their start and end apart: 30, of which 13 were waited for; matrix products, arithmetic and copies ran while one was open for 22% of the time, Pallas kernels for 0%

profile of v1, /device:TPU:8, one launch (start us, length us, event | category | flops | bytes accessed | tf_op | source)
XLA Modules:
  0.0 291.1 jit_solution(13664539563304978944)
XLA Ops:
  0.0 1.1 copy-done
  1.1 29.3 %all_gather.10 = bf16[768,384]{1,0:T(8,128)(2,1)S(1)} all-gather(bf16[96,384]{1,0:T(8,128)(2,1)S(1)} %constant_dynamic-slice_fusion.1), channel_id=1, replica_groups=mesh['blk'=8,'head'=8,'bend'=4] {'head'}, dimensions={0}, use_global_device_ids=true | all-gather | bytes 663552 | tf_op jit(solution)/shard_map/all_gather | solution.py:95
  30.3 1.5 collective-permute-start.14
  31.8 1.7 collective-permute-start.15
  33.6 1.0 constant_dynamic-slice_fusion
  34.7 27.8 %all_gather.11 = bf16[3072,96]{0,1:T(8,128)(2,1)} all-gather(bf16[384,96]{0,1:T(8,128)(2,1)S(1)} %copy.20), channel_id=1, replica_groups=mesh['blk'=8,'head'=8,'bend'=4] {'head'}, dimensions={0}, use_global_device_ids=true | all-gather | bytes 663552 | tf_op jit(solution)/shard_map/all_gather | solution.py:95
  63.5 24.7 %all_gather.9 = bf16[768,96]{1,0:T(8,128)(2,1)S(1)} all-gather(bf16[96,96]{1,0:T(8,128)(2,1)S(1)} %constant_dynamic-slice_fusion.2), channel_id=1, replica_groups=mesh['blk'=8,'head'=8,'bend'=4] {'head'}, dimensions={0}, use_global_device_ids=true | all-gather | bytes 165888 | tf_op jit(solution)/shard_map/all_gather | solution.py:95
  88.3 1.6 collective-permute-start.6
  90.8 1.3 gather_fusion
  92.1 1.9 bitcast_dynamic-update-slice_fusion.7
  95.5 4.4 %stack.112 = pred[7]{0:T(512)(128)(4,1)S(1)} concatenate(pred[1]{0:T(512)(128)(4,1)} %bitcast.2, pred[1]{0:T(512)(128)(4,1)} %bitcast.4, pred[1]{0:T(512)(128)(4,1)} %bitcast.6, pred[1]{0:T(512)(128)(4,1)} %bitcast.8, pred[1]{0:T(512)(128)(4,1)} %bitcast.10, pred[1]{0:T(512)(128)(4,1)} %bitcast.12, pred[1]{0:T(512)(128)(4,1)} %bitcast.14), dimensions={0} | concatenate | bytes 14 | tf_op jit(solution)/shard_map/stack | solution.py:158
  100.6 1.8 collective-permute-start.7
  102.4 3.4 %collective-permute-done.7 = bf16[768,96]{0,1:T(8,128)(2,1)S(1)} collective-permute-done((bf16[768,96]{0,1:T(8,128)(2,1)S(1)}, bf16[768,96]{0,1:T(8,128)(2,1)S(1)}, u32[]{:S(2)}, u32[]{:S(2)}) %collective-permute-start.7) | collective-permute-done | bytes 147488 | tf_op jit(solution)/shard_map/ppermute | solution.py:26
  105.8 1.5 collective-permute-start.8
  107.3 4.1 %collective-permute-done.8 = bf16[384,96]{0,1:T(8,128)(2,1)S(1)} collective-permute-done((bf16[384,96]{0,1:T(8,128)(2,1)S(1)}, bf16[384,96]{0,1:T(8,128)(2,1)S(1)}, u32[]{:S(2)}, u32[]{:S(2)}) %collective-permute-start.8) | collective-permute-done | bytes 73760 | tf_op jit(solution)/shard_map/ppermute | solution.py:26
  111.4 1.7 collective-permute-start.9
  113.1 2.6 collective-permute-done.9
  115.8 1.3 collective-permute-done.10
  117.2 1.2 collective-permute-done.11
  118.6 1.2 collective-permute-done.12
  120.0 1.2 collective-permute-done.13
  121.2 3.0 %collective-permute-start.23 = (bf16[3072,96]{0,1:T(8,128)(2,1)}, bf16[3072,96]{0,1:T(8,128)(2,1)}, u32[]{:S(2)}, u32[]{:S(2)}) collective-permute-start(bf16[3072,96]{0,1:T(8,128)(2,1)} %all_gather.11), channel_id=1, source_target_pairs={{0,96},{32,0},{64,32},{96,64},{128,224},{160,128},{192,160},{224,1... | collective-permute-start | bytes 1769480 | tf_op jit(solution)/shard_map/ppermute | solution.py:26
  125.1 1.9 bitcast_dynamic-update-slice_fusion.6
  127.1 10.3 %collective-permute-done.23 = bf16[3072,96]{0,1:T(8,128)(2,1)} collective-permute-done((bf16[3072,96]{0,1:T(8,128)(2,1)}, bf16[3072,96]{0,1:T(8,128)(2,1)}, u32[]{:S(2)}, u32[]{:S(2)}) %collective-permute-start.23) | collective-permute-done | bytes 589856 | tf_op jit(solution)/shard_map/ppermute | solution.py:26
  138.3 1.9 bitcast_dynamic-update-slice_fusion.5
  140.2 1.0 slice.36
  141.3 2.0 bitcast_dynamic-update-slice_fusion.14
  143.3 1.0 slice.37
  144.3 3.8 %collective-permute-start.25 = (bf16[1536,96]{0,1:T(8,128)(2,1)S(1)}, bf16[1536,96]{0,1:T(8,128)(2,1)S(1)}, u32[]{:S(2)}, u32[]{:S(2)}) collective-permute-start(bf16[1536,96]{0,1:T(8,128)(2,1)S(1)} %slice.37), channel_id=1, source_target_pairs={{0,96},{32,0},{64,32},{96,64},{128,224},{160,128},{192,160},{224,1... | collective-permute-start | bytes 884744 | tf_op jit(solution)/shard_map/ppermute | solution.py:26
  148.0 2.0 bitcast_dynamic-update-slice_fusion.13
  150.0 1.0 slice.34
  151.0 1.0 slice.35
  152.0 15.7 %collective-permute-done.24 = bf16[1536,96]{0,1:T(8,128)(2,1)S(1)} collective-permute-done((bf16[1536,96]{0,1:T(8,128)(2,1)S(1)}, bf16[1536,96]{0,1:T(8,128)(2,1)S(1)}, u32[]{:S(2)}, u32[]{:S(2)}) %collective-permute-start.24) | collective-permute-done | bytes 294944 | tf_op jit(solution)/shard_map/ppermute | solution.py:26
  168.8 3.2 %collective-permute-start.17 = (bf16[384,384]{1,0:T(8,128)(2,1)S(1)}, bf16[384,384]{1,0:T(8,128)(2,1)S(1)}, u32[]{:S(2)}, u32[]{:S(2)}) collective-permute-start(bf16[384,384]{1,0:T(8,128)(2,1)S(1)} %slice.35), channel_id=1, source_target_pairs={{0,96},{32,0},{64,32},{96,64},{128,224},{160,128},{192,160},{224,1... | collective-permute-start | bytes 884744 | tf_op jit(solution)/shard_map/ppermute | solution.py:26
  172.8 5.1 %collective-permute-done.16 = bf16[384,384]{1,0:T(8,128)(2,1)S(1)} collective-permute-done((bf16[384,384]{1,0:T(8,128)(2,1)S(1)}, bf16[384,384]{1,0:T(8,128)(2,1)S(1)}, u32[]{:S(2)}, u32[]{:S(2)}) %collective-permute-start.16) | collective-permute-done | bytes 294944 | tf_op jit(solution)/shard_map/ppermute | solution.py:26
  179.6 1.9 bitcast_dynamic-update-slice_fusion.11
  182.0 5.3 %collective-permute-done.1.refs_2_ = bf16[2,256,768]{2,1,0:T(8,128)(2,1)} collective-permute-done((bf16[2,256,768]{2,1,0:T(8,128)(2,1)S(1)}, bf16[2,256,768]{2,1,0:T(8,128)(2,1)}, u32[]{:S(2)}, u32[]{:S(2)}) %collective-permute-start.1) | collective-permute-done | bytes 786464 | tf_op jit(solution)/shard_map/ppermute | solution.py:18
  187.3 7.7 %collective-permute-start.3 = (bf16[2,256,768]{2,1,0:T(8,128)(2,1)}, bf16[2,256,768]{2,1,0:T(8,128)(2,1)}, u32[]{:S(2)}, u32[]{:S(2)}) collective-permute-start(bf16[2,256,768]{2,1,0:T(8,128)(2,1)} %collective-permute-done.1.refs_2_), channel_id=1, source_target_pairs={{0,252},{4,0},{8,4},{12,8},{16,12},{20,16},{24,20},{28,24},{32,28}... | collective-permute-start | bytes 2359304 | tf_op jit(solution)/shard_map/ppermute | solution.py:18
  200.0 5.8 %gather_fusion.2 = bf16[8,768,384]{2,1,0:T(8,128)(2,1)} fusion(bf16[8,768,384]{2,1,0:T(8,128)(2,1)} %bitcast_dynamic-update-slice_fusion.8, s32[1024]{0:T(1024)S(1)} %pad_clamp_fusion), kind=kCustom, calls=%fused_computation.2 | custom fusion | bytes 9437216 | tf_op jit(solution)/shard_map/jit(_take)/gather | solution.py:113
  205.8 5.1 %select_bitcast_fusion = bf16[768,8,384]{2,0,1:T(8,128)(2,1)} fusion(bf16[8,768,384]{2,1,0:T(8,128)(2,1)} %gather_fusion.2, pred[8]{0:T(512)(128)(4,1)S(1)} %compare_and_fusion), kind=kLoop, calls=%fused_computation.5 | loop fusion | flops 2359296 | bytes 9437192 | tf_op jit(solution)/shard_map/jit(_take)/select_n | solution.py:113
  210.9 6.6 %copy.18 = bf16[768,8,384]{0,2,1:T(8,128)(2,1)} copy(bf16[768,8,384]{2,0,1:T(8,128)(2,1)} %select_bitcast_fusion) | data formatting | bytes 9437184 | tf_op jit(solution)/shard_map/jit(_take)/select_n | solution.py:113
  218.5 5.4 %gather_fusion.3 = bf16[8,3072,96]{1,2,0:T(8,128)(2,1)} fusion(bf16[8,3072,96]{1,2,0:T(8,128)(2,1)} %bitcast_dynamic-update-slice_fusion, s32[1024]{0:T(1024)S(1)} %pad_clamp_fusion), kind=kCustom, calls=%fused_computation.3 | custom fusion | bytes 9437216 | tf_op jit(solution)/shard_map/jit(_take)/gather | solution.py:113
  223.9 7.7 %collective-permute-start.5 = (bf16[2,256,768]{2,1,0:T(8,128)(2,1)}, bf16[2,256,768]{2,1,0:T(8,128)(2,1)}, u32[]{:S(2)}, u32[]{:S(2)}) collective-permute-start(bf16[2,256,768]{2,1,0:T(8,128)(2,1)} %collective-permute-done.3.refs_4_), channel_id=1, source_target_pairs={{0,252},{4,0},{8,4},{12,8},{16,12},{20,16},{24,20},{28,24},{32,28}... | collective-permute-start | bytes 2359304 | tf_op jit(solution)/shard_map/ppermute | solution.py:18
  231.6 5.1 %broadcast_select_fusion = bf16[8,3072,96]{1,2,0:T(8,128)(2,1)} fusion(bf16[8,3072,96]{1,2,0:T(8,128)(2,1)} %gather_fusion.3, pred[8]{0:T(512)(128)(4,1)S(1)} %compare_and_fusion), kind=kLoop, calls=%fused_computation.6 | loop fusion | flops 2359296 | bytes 9437192 | tf_op jit(solution)/shard_map/jit(_take)/select_n | solution.py:113
  236.7 12.6 %collective-permute-done.4.refs_5_ = bf16[2,256,768]{2,1,0:T(8,128)(2,1)S(1)} collective-permute-done((bf16[2,256,768]{2,1,0:T(8,128)(2,1)}, bf16[2,256,768]{2,1,0:T(8,128)(2,1)S(1)}, u32[]{:S(2)}, u32[]{:S(2)}) %collective-permute-start.4) | collective-permute-done | bytes 786464 | tf_op jit(solution)/shard_map/ppermute | solution.py:18
  250.2 31.9 %shard_map.100 = bf16[256,768]{1,0:T(8,128)(2,1)} custom-call(s32[7]{0:T(128)} %convert_element_type.16.mask_ref, bf16[256,768]{1,0:T(8,128)(2,1)} %q_ref.1, bf16[2,256,768]{2,1,0:T(8,128)(2,1)} %refs_0_.1, bf16[2,256,768]{2,1,0:T(8,128)(2,1)} %collective-permute-done.refs_1_, bf16[2,256,768]{2,1,0:T(8,128)(2,1)} %collective-permute-done.1.refs_2_, ...), custom_call_target="tpu_custom_call" | custom-call | flops 1409286144 | bytes 6291456 | tf_op jit(solution)/shard_map/pallas_call | solution.py:82
  282.1 1.6 multiply_reduce_fusion
  283.7 7.3 %fusion.17 = bf16[256,768]{1,0:T(8,128)(2,1)} fusion(f32[256,768]{1,0:T(8,128)S(1)} %get-tuple-element.13, bf16[3072,768]{0,1:T(8,128)(2,1)} %bitcast.106, bf16[768,3072]{0,1:T(8,128)(2,1)} %bitcast.105, f32[768]{0:T(1024)S(1)} %copy-done.5, f32[256]{0:T(256)S(1)} %add_rsqrt_fusion), kind=kOutput, calls=%fused_computation.22 | convolution fusion | flops 2423980032 | bytes 10620928 | tf_op jit(solution)/shard_map/dot_general | solution.py:168
  (88 shorter events, 16.8 us)
Async XLA Ops:
  0.0 1.1 copy-start
  0.0 94.8 %copy-start.2 = (s32[1,4]{1,0:T(1,128)S(1)}, s32[1,4]{1,0:T(1,128)}, u32[]{:S(2)}) copy-start(s32[1,4]{1,0:T(1,128)} %param.17) | copy-start | bytes 52
  30.3 110.9 %collective-permute-start.14 = (bf16[768,384]{1,0:T(8,128)(2,1)S(1)}, bf16[768,384]{1,0:T(8,128)(2,1)}, u32[]{:S(2)}, u32[]{:S(2)}) collective-permute-start(bf16[768,384]{1,0:T(8,128)(2,1)S(1)} %all_gather.10), channel_id=1, source_target_pairs={{0,32},{32,64},{64,96},{96,0},{128,160},{160,192},{192,224},{224,1... | collective-permute-start | bytes 1769480 | tf_op jit(solution)/shard_map/ppermute | solution.py:26
  31.8 112.4 %collective-permute-start.15 = (bf16[768,384]{1,0:T(8,128)(2,1)S(1)}, bf16[768,384]{1,0:T(8,128)(2,1)}, u32[]{:S(2)}, u32[]{:S(2)}) collective-permute-start(bf16[768,384]{1,0:T(8,128)(2,1)S(1)} %all_gather.10), channel_id=1, source_target_pairs={{0,96},{32,0},{64,32},{96,64},{128,224},{160,128},{192,160},{224,1... | collective-permute-start | bytes 1769480 | tf_op jit(solution)/shard_map/ppermute | solution.py:26
  33.6 146.0 %collective-permute-start.18 = (bf16[768,384]{1,0:T(8,128)(2,1)S(1)}, bf16[768,384]{1,0:T(8,128)(2,1)}, u32[]{:S(2)}, u32[]{:S(2)}) collective-permute-start(bf16[768,384]{1,0:T(8,128)(2,1)S(1)} %all_gather.10), channel_id=1, source_target_pairs={{0,1},{1,0},{2,3},{3,2},{4,5},{5,4},{6,7},{7,6},{8,9},{9,8},{10,11... | collective-permute-start | bytes 1769480 | tf_op jit(solution)/shard_map/ppermute | solution.py:31
  62.5 62.5 %collective-permute-start.22 = (bf16[3072,96]{0,1:T(8,128)(2,1)}, bf16[3072,96]{0,1:T(8,128)(2,1)}, u32[]{:S(2)}, u32[]{:S(2)}) collective-permute-start(bf16[3072,96]{0,1:T(8,128)(2,1)} %all_gather.11), channel_id=1, source_target_pairs={{0,32},{32,64},{64,96},{96,0},{128,160},{160,192},{192,224},{224,1... | collective-permute-start | bytes 1769480 | tf_op jit(solution)/shard_map/ppermute | solution.py:26
  88.3 12.3 %collective-permute-start.6 = (bf16[768,96]{0,1:T(8,128)(2,1)S(1)}, bf16[768,96]{0,1:T(8,128)(2,1)S(1)}, u32[]{:S(2)}, u32[]{:S(2)}) collective-permute-start(bf16[768,96]{0,1:T(8,128)(2,1)S(1)} %copy.14), channel_id=1, source_target_pairs={{0,32},{32,64},{64,96},{96,0},{128,160},{160,192},{192,224},{224,1... | collective-permute-start | bytes 442376 | tf_op jit(solution)/shard_map/ppermute | solution.py:26
  100.6 5.2 %collective-permute-start.7 = (bf16[768,96]{0,1:T(8,128)(2,1)S(1)}, bf16[768,96]{0,1:T(8,128)(2,1)S(1)}, u32[]{:S(2)}, u32[]{:S(2)}) collective-permute-start(bf16[768,96]{0,1:T(8,128)(2,1)S(1)} %copy.14), channel_id=1, source_target_pairs={{0,96},{32,0},{64,32},{96,64},{128,224},{160,128},{192,160},{224,1... | collective-permute-start | bytes 442376 | tf_op jit(solution)/shard_map/ppermute | solution.py:26
  105.8 5.6 %collective-permute-start.8 = (bf16[384,96]{0,1:T(8,128)(2,1)S(1)}, bf16[384,96]{0,1:T(8,128)(2,1)S(1)}, u32[]{:S(2)}, u32[]{:S(2)}) collective-permute-start(bf16[384,96]{0,1:T(8,128)(2,1)S(1)} %slice.32), channel_id=1, source_target_pairs={{0,32},{32,64},{64,96},{96,0},{128,160},{160,192},{192,224},{224,1... | collective-permute-start | bytes 221192 | tf_op jit(solution)/shard_map/ppermute | solution.py:26
  111.4 4.4 %collective-permute-start.9 = (bf16[384,96]{0,1:T(8,128)(2,1)S(1)}, bf16[384,96]{0,1:T(8,128)(2,1)S(1)}, u32[]{:S(2)}, u32[]{:S(2)}) collective-permute-start(bf16[384,96]{0,1:T(8,128)(2,1)S(1)} %slice.33), channel_id=1, source_target_pairs={{0,96},{32,0},{64,32},{96,64},{128,224},{160,128},{192,160},{224,1... | collective-permute-start | bytes 221192 | tf_op jit(solution)/shard_map/ppermute | solution.py:26
  115.7 1.4 collective-permute-start.10
  117.1 1.4 collective-permute-start.11
  118.5 1.4 collective-permute-start.12
  119.8 1.4 collective-permute-start.13
  121.2 16.2 %collective-permute-start.23 = (bf16[3072,96]{0,1:T(8,128)(2,1)}, bf16[3072,96]{0,1:T(8,128)(2,1)}, u32[]{:S(2)}, u32[]{:S(2)}) collective-permute-start(bf16[3072,96]{0,1:T(8,128)(2,1)} %all_gather.11), channel_id=1, source_target_pairs={{0,96},{32,0},{64,32},{96,64},{128,224},{160,128},{192,160},{224,1... | collective-permute-start | bytes 1769480 | tf_op jit(solution)/shard_map/ppermute | solution.py:26
  124.8 42.9 %copy-start.3 = (bf16[2,256,768]{2,1,0:T(8,128)(2,1)S(1)}, bf16[2,256,768]{2,1,0:T(8,128)(2,1)}, u32[]{:S(2)}) copy-start(bf16[2,256,768]{2,1,0:T(8,128)(2,1)} %refs_0_.1) | copy-start | bytes 2359300
  125.0 43.7 %collective-permute-start.26 = (bf16[3072,96]{0,1:T(8,128)(2,1)}, bf16[3072,96]{0,1:T(8,128)(2,1)S(1)}, u32[]{:S(2)}, u32[]{:S(2)}) collective-permute-start(bf16[3072,96]{0,1:T(8,128)(2,1)} %all_gather.11), channel_id=1, source_target_pairs={{0,1},{1,0},{2,3},{3,2},{4,5},{5,4},{6,7},{7,6},{8,9},{9,8},{10,11... | collective-permute-start | bytes 1769480 | tf_op jit(solution)/shard_map/ppermute | solution.py:31
  137.4 44.2 %collective-permute-start = (bf16[2,256,768]{2,1,0:T(8,128)(2,1)}, bf16[2,256,768]{2,1,0:T(8,128)(2,1)}, u32[]{:S(2)}, u32[]{:S(2)}) collective-permute-start(bf16[2,256,768]{2,1,0:T(8,128)(2,1)} %refs_0_.1), channel_id=1, source_target_pairs={{0,4},{4,8},{8,12},{12,16},{16,20},{20,24},{24,28},{28,32},{32,36}... | collective-permute-start | bytes 2359304 | tf_op jit(solution)/shard_map/ppermute | solution.py:18
  141.2 26.5 %collective-permute-start.24 = (bf16[1536,96]{0,1:T(8,128)(2,1)S(1)}, bf16[1536,96]{0,1:T(8,128)(2,1)S(1)}, u32[]{:S(2)}, u32[]{:S(2)}) collective-permute-start(bf16[1536,96]{0,1:T(8,128)(2,1)S(1)} %slice.36), channel_id=1, source_target_pairs={{0,32},{32,64},{64,96},{96,0},{128,160},{160,192},{192,224},{224,1... | collective-permute-start | bytes 884744 | tf_op jit(solution)/shard_map/ppermute | solution.py:26
  144.3 23.5 %collective-permute-start.25 = (bf16[1536,96]{0,1:T(8,128)(2,1)S(1)}, bf16[1536,96]{0,1:T(8,128)(2,1)S(1)}, u32[]{:S(2)}, u32[]{:S(2)}) collective-permute-start(bf16[1536,96]{0,1:T(8,128)(2,1)S(1)} %slice.37), channel_id=1, source_target_pairs={{0,96},{32,0},{64,32},{96,64},{128,224},{160,128},{192,160},{224,1... | collective-permute-start | bytes 884744 | tf_op jit(solution)/shard_map/ppermute | solution.py:26
  167.7 19.6 %collective-permute-start.1 = (bf16[2,256,768]{2,1,0:T(8,128)(2,1)S(1)}, bf16[2,256,768]{2,1,0:T(8,128)(2,1)}, u32[]{:S(2)}, u32[]{:S(2)}) collective-permute-start(bf16[2,256,768]{2,1,0:T(8,128)(2,1)S(1)} %copy-done.3), channel_id=1, source_target_pairs={{0,252},{4,0},{8,4},{12,8},{16,12},{20,16},{24,20},{28,24},{32,28}... | collective-permute-start | bytes 2359304 | tf_op jit(solution)/shard_map/ppermute | solution.py:18
  167.8 10.2 %collective-permute-start.16 = (bf16[384,384]{1,0:T(8,128)(2,1)S(1)}, bf16[384,384]{1,0:T(8,128)(2,1)S(1)}, u32[]{:S(2)}, u32[]{:S(2)}) collective-permute-start(bf16[384,384]{1,0:T(8,128)(2,1)S(1)} %slice.34), channel_id=1, source_target_pairs={{0,32},{32,64},{64,96},{96,0},{128,160},{160,192},{192,224},{224,1... | collective-permute-start | bytes 884744 | tf_op jit(solution)/shard_map/ppermute | solution.py:26
  168.8 9.4 %collective-permute-start.17 = (bf16[384,384]{1,0:T(8,128)(2,1)S(1)}, bf16[384,384]{1,0:T(8,128)(2,1)S(1)}, u32[]{:S(2)}, u32[]{:S(2)}) collective-permute-start(bf16[384,384]{1,0:T(8,128)(2,1)S(1)} %slice.35), channel_id=1, source_target_pairs={{0,96},{32,0},{64,32},{96,64},{128,224},{160,128},{192,160},{224,1... | collective-permute-start | bytes 884744 | tf_op jit(solution)/shard_map/ppermute | solution.py:26
  178.0 9.3 %collective-permute-start.19 = (bf16[768,384]{1,0:T(8,128)(2,1)}, bf16[768,384]{1,0:T(8,128)(2,1)S(1)}, u32[]{:S(2)}, u32[]{:S(2)}) collective-permute-start(bf16[768,384]{1,0:T(8,128)(2,1)} %collective-permute-done.14), channel_id=1, source_target_pairs={{0,1},{1,0},{2,3},{3,2},{4,5},{5,4},{6,7},{7,6},{8,9},{9,8},{10,11... | collective-permute-start | bytes 1769480 | tf_op jit(solution)/shard_map/ppermute | solution.py:31
  178.1 17.8 %collective-permute-start.20 = (bf16[768,384]{1,0:T(8,128)(2,1)}, bf16[768,384]{1,0:T(8,128)(2,1)S(1)}, u32[]{:S(2)}, u32[]{:S(2)}) collective-permute-start(bf16[768,384]{1,0:T(8,128)(2,1)} %collective-permute-done.15), channel_id=1, source_target_pairs={{0,1},{1,0},{2,3},{3,2},{4,5},{5,4},{6,7},{7,6},{8,9},{9,8},{10,11... | collective-permute-start | bytes 1769480 | tf_op jit(solution)/shard_map/ppermute | solution.py:31
  179.5 17.2 %collective-permute-start.27 = (bf16[3072,96]{0,1:T(8,128)(2,1)}, bf16[3072,96]{0,1:T(8,128)(2,1)S(1)}, u32[]{:S(2)}, u32[]{:S(2)}) collective-permute-start(bf16[3072,96]{0,1:T(8,128)(2,1)} %collective-permute-done.22), channel_id=1, source_target_pairs={{0,1},{1,0},{2,3},{3,2},{4,5},{5,4},{6,7},{7,6},{8,9},{9,8},{10,11... | collective-permute-start | bytes 1769480 | tf_op jit(solution)/shard_map/ppermute | solution.py:31
  181.5 16.7 %collective-permute-start.28 = (bf16[3072,96]{0,1:T(8,128)(2,1)}, bf16[3072,96]{0,1:T(8,128)(2,1)S(1)}, u32[]{:S(2)}, u32[]{:S(2)}) collective-permute-start(bf16[3072,96]{0,1:T(8,128)(2,1)} %collective-permute-done.23), channel_id=1, source_target_pairs={{0,1},{1,0},{2,3},{3,2},{4,5},{5,4},{6,7},{7,6},{8,9},{9,8},{10,11... | collective-permute-start | bytes 1769480 | tf_op jit(solution)/shard_map/ppermute | solution.py:31
  187.3 36.6 %collective-permute-start.2 = (bf16[2,256,768]{2,1,0:T(8,128)(2,1)}, bf16[2,256,768]{2,1,0:T(8,128)(2,1)}, u32[]{:S(2)}, u32[]{:S(2)}) collective-permute-start(bf16[2,256,768]{2,1,0:T(8,128)(2,1)} %collective-permute-done.refs_1_), channel_id=1, source_target_pairs={{0,4},{4,8},{8,12},{12,16},{16,20},{20,24},{24,28},{28,32},{32,36}... | collective-permute-start | bytes 2359304 | tf_op jit(solution)/shard_map/ppermute | solution.py:18
  187.3 36.6 %collective-permute-start.3 = (bf16[2,256,768]{2,1,0:T(8,128)(2,1)}, bf16[2,256,768]{2,1,0:T(8,128)(2,1)}, u32[]{:S(2)}, u32[]{:S(2)}) collective-permute-start(bf16[2,256,768]{2,1,0:T(8,128)(2,1)} %collective-permute-done.1.refs_2_), channel_id=1, source_target_pairs={{0,252},{4,0},{8,4},{12,8},{16,12},{20,16},{24,20},{28,24},{32,28}... | collective-permute-start | bytes 2359304 | tf_op jit(solution)/shard_map/ppermute | solution.py:18
  195.9 3.2 %collective-permute-start.21 = (bf16[768,384]{1,0:T(8,128)(2,1)S(1)}, bf16[768,384]{1,0:T(8,128)(2,1)S(1)}, u32[]{:S(2)}, u32[]{:S(2)}) collective-permute-start(bf16[768,384]{1,0:T(8,128)(2,1)S(1)} %constant_dynamic-update-slice_fusion.2), channel_id=1, source_target_pairs={{0,1},{1,0},{2,3},{3,2},{4,5},{5,4},{6,7},{7,6},{8,9},{9,8},{10,11... | collective-permute-start | bytes 1769480 | tf_op jit(solution)/shard_map/ppermute | solution.py:31
  196.8 20.8 %collective-permute-start.29 = (bf16[3072,96]{0,1:T(8,128)(2,1)S(1)}, bf16[3072,96]{0,1:T(8,128)(2,1)S(1)}, u32[]{:S(2)}, u32[]{:S(2)}) collective-permute-start(bf16[3072,96]{0,1:T(8,128)(2,1)S(1)} %constant_dynamic-update-slice_fusion.4), channel_id=1, source_target_pairs={{0,1},{1,0},{2,3},{3,2},{4,5},{5,4},{6,7},{7,6},{8,9},{9,8},{10,11... | collective-permute-start | bytes 1769480 | tf_op jit(solution)/shard_map/ppermute | solution.py:31
  223.9 25.4 %collective-permute-start.4 = (bf16[2,256,768]{2,1,0:T(8,128)(2,1)}, bf16[2,256,768]{2,1,0:T(8,128)(2,1)S(1)}, u32[]{:S(2)}, u32[]{:S(2)}) collective-permute-start(bf16[2,256,768]{2,1,0:T(8,128)(2,1)} %collective-permute-done.2.refs_3_), channel_id=1, source_target_pairs={{0,4},{4,8},{8,12},{12,16},{16,20},{20,24},{24,28},{28,32},{32,36}... | collective-permute-start | bytes 2359304 | tf_op jit(solution)/shard_map/ppermute | solution.py:18
  223.9 25.4 %collective-permute-start.5 = (bf16[2,256,768]{2,1,0:T(8,128)(2,1)}, bf16[2,256,768]{2,1,0:T(8,128)(2,1)}, u32[]{:S(2)}, u32[]{:S(2)}) collective-permute-start(bf16[2,256,768]{2,1,0:T(8,128)(2,1)} %collective-permute-done.3.refs_4_), channel_id=1, source_target_pairs={{0,252},{4,0},{8,4},{12,8},{16,12},{20,16},{24,20},{28,24},{32,28}... | collective-permute-start | bytes 2359304 | tf_op jit(solution)/shard_map/ppermute | solution.py:18
  236.7 45.4 %copy-start.1 = (bf16[256,768]{1,0:T(8,128)(2,1)S(1)}, bf16[256,768]{1,0:T(8,128)(2,1)}, u32[]{:S(2)}) copy-start(bf16[256,768]{1,0:T(8,128)(2,1)} %param.12) | copy-start | bytes 1179652
  236.7 47.0 %copy-start.5 = (f32[768]{0:T(1024)S(1)}, f32[768]{0:T(1024)}, u32[]{:S(2)}) copy-start(f32[768]{0:T(1024)} %param.16) | copy-start | bytes 9220
  249.3 0.9 copy-start.4
